TPU v7x, 256 devices: a whole 4x4x8 slice. The times are simulated.
256 devices in a mesh: dp: 32 (over y, x, z_lo), tensor: 8 (over z_hi, core).
Axes of the slice: x: 4, y: 4, z: 8 (z_hi: 4, z_lo: 2; z = z_hi * 2 + z_lo), core: 2. Of those that a mesh axis runs over, the one named last changes fastest.
Arguments:
- grad_out: bfloat16 [24576, 4096], P(('dp', 'tensor')), may hold values from -0.15625 to 0.15625
- activations: bfloat16 [24576, 14336], P('dp', 'tensor'), may hold values from -6 to 6
- grad_dither: float32 [24576, 4096], P(('dp', 'tensor')), may hold values from -0.5 to 0.5
- hidden_dither: float32 [32, 14336], P('dp', 'tensor'), may hold values from -0.25 to 0.25
- feature_dither: float32 [32, 4096], P('dp'), may hold values from -0.25 to 0.25
Outputs:
- weight_grad: float32 [4096, 14336], P('dp', 'tensor')
All inputs are finite; a program needn't handle non-finite values.
Results may differ from a plain program's by a relative error of at most 0.014.
Values may be sent and summed in bfloat16 or wider, within the bound.
A program may use at most 128 MiB of HBM per device.

v0:
```python
import jax
import jax.numpy as jnp
from jax import lax
from jax.sharding import PartitionSpec as P

BLOCK = 128
Y_LEVELS = 8
W_LEVELS = 7
COL_CHUNKS = 2
epsilon = 1e-06


def code_rows(grad_out, grad_dither):
    row_count, feat_width = grad_out.shape
    block_count = feat_width // BLOCK
    grad_float = grad_out.astype(jnp.float32).reshape(row_count, block_count, BLOCK)
    magnitude = jnp.max(jnp.abs(grad_float), axis=2)
    y_scale = ((magnitude + epsilon) / Y_LEVELS).astype(jnp.bfloat16)
    scaled = grad_float / y_scale.astype(jnp.float32)[:, :, None]
    y_code = (scaled.reshape(row_count, feat_width) + grad_dither).astype(jnp.bfloat16)
    held = lax.optimization_barrier(y_code).astype(jnp.float32)
    values = held.reshape(row_count, block_count, BLOCK) * y_scale.astype(jnp.float32)[:, :, None]
    return values.reshape(row_count, feat_width).astype(jnp.bfloat16)


def group_terms(partial_value, feature_part, hidden_part):
    feat_rows, unit_cols = partial_value.shape
    block_count = feat_rows // BLOCK
    blocks = partial_value.reshape(block_count, BLOCK, unit_cols)
    magnitude = jnp.max(jnp.abs(blocks), axis=1)
    block_scale = ((magnitude + epsilon) / W_LEVELS).astype(jnp.bfloat16)
    scaled = (blocks / block_scale.astype(jnp.float32)[:, None, :]).reshape(feat_rows, unit_cols)
    code_block = (scaled + hidden_part[None, :] + feature_part[:, None]).astype(jnp.bfloat16)
    held = lax.optimization_barrier(code_block).astype(jnp.float32)
    values = (
        held.reshape(block_count, BLOCK, unit_cols) * block_scale.astype(jnp.float32)[:, None, :]
    )
    return values.reshape(feat_rows, unit_cols).astype(jnp.bfloat16)


def per_device(grad_out, activations, grad_dither, hidden_dither, feature_dither):
    feat_width = grad_out.shape[1]
    y_local = code_rows(grad_out, grad_dither)
    y_hat = lax.all_gather(y_local, "tensor", axis=0, tiled=True)
    unit_count = activations.shape[1]
    owners = lax.axis_size("dp")
    own_rows = feat_width // owners
    hidden_noise = hidden_dither[0]
    feature_noise = feature_dither[0]
    width = unit_count // COL_CHUNKS
    sums = []
    for chunk in range(COL_CHUNKS):
        cols = slice(chunk * width, (chunk + 1) * width)
        partial_value = lax.dot_general(
            y_hat,
            activations[:, cols],
            (((0,), (0,)), ((), ())),
            preferred_element_type=jnp.float32,
        )
        terms = group_terms(partial_value, feature_noise, hidden_noise[cols])
        arrived = lax.all_to_all(terms, "dp", split_axis=0, concat_axis=0, tiled=True)
        held = lax.optimization_barrier(arrived).astype(jnp.float32)
        sums.append(jnp.sum(held.reshape(owners, own_rows, width), axis=0))
    return jnp.concatenate(sums, axis=1)


def solution(mesh):
    placed = (
        P(("dp", "tensor"), None),
        P("dp", "tensor"),
        P(("dp", "tensor"), None),
        P("dp", "tensor"),
        P("dp", None),
    )
    return jax.shard_map(
        per_device, mesh=mesh, in_specs=placed, out_specs=P("dp", "tensor"), check_vma=False
    )
```

profile of v0, /device:TPU:38, one launch (start us, length us, event | category | flops | bytes accessed | tf_op | source)
XLA Modules:
  0.0 383.4 jit_solution(3777527201818774682)
XLA Ops:
  6.5 0.0 copy-start
  6.5 0.0 all-gather.2.cloned.1.call-start
  6.5 1.4 fusion.8
  7.9 0.0 copy-start.2
  7.9 0.3 copy.6
  8.2 0.5 reduce_max.27
  8.7 0.5 div.47
  9.2 0.0 copy-done
  9.2 2.5 fusion.10
  11.7 1.8 fusion.11
  13.5 0.0 all-gather.2.cloned.1.call-update
  13.5 0.0 copy-done.2
  13.6 0.0 copy-start.4
  13.6 72.3 %all-gather.2.cloned.1.call-done = bf16[768,4096]{1,0:T(8,128)(2,1)} async-done(((bf16[96,4096]{1,0:T(8,128)(2,1)}), bf16[768,4096]{1,0:T(8,128)(2,1)}) %all-gather.2.cloned.1.call-update) | async-done | bytes 6291472 | tf_op jit(solution)/shard_map/all_gather | solution.py:44
  85.9 0.0 copy-start.3
  85.9 10.0 %bitcast_reduce_fusion = (f32[32,896]{1,0:T(8,128)S(1)}, f32[4096,896]{1,0:T(8,128)S(1)}) fusion(bf16[768,4096]{1,0:T(8,128)(2,1)} %all-gather.2.cloned.1.call-done, bf16[768,1792]{1,0:T(8,128)(2,1)} %param.6), kind=kOutput, calls=%fused_computation.14 | convolution fusion | flops 5644455936 | bytes 22462464 | tf_op jit(solution)/shard_map/dot_general | solution.py:54
  95.9 0.0 copy-done.4
  95.9 0.0 copy-done.3
  95.9 0.0 copy-start.1
  95.9 10.3 %bitcast_reduce_fusion.1 = (f32[32,896]{1,0:T(8,128)S(1)}, f32[4096,896]{1,0:T(8,128)}) fusion(bf16[768,4096]{1,0:T(8,128)(2,1)S(1)} %copy-done.3, bf16[768,1792]{1,0:T(8,128)(2,1)S(1)} %copy-done.4), kind=kOutput, calls=%fused_computation.15 | convolution fusion | flops 5644455936 | bytes 22462464 | tf_op jit(solution)/shard_map/dot_general | solution.py:54
  106.3 0.0 copy-done.1
  106.3 10.0 %fusion.2 = (bf16[4096,896]{1,0:T(8,128)(2,1)}, bf16[4096,896]{1,0:T(8,128)(2,1)S(1)}) fusion(f32[4096,896]{1,0:T(8,128)} %get-tuple-element.10, f32[4096]{0:T(1024)S(1)} %bitcast.51, f32[896]{0:T(1024)S(1)} %get-tuple-element.5, f32[32,896]{1,0:T(8,128)S(1)} %get-tuple-element.13, f32[896]{0:T(1024)S(1)} %get-tuple-element.6, ...), kind=kLoop, calls=%fused_computation.6 | loop fusion | flops 29360128 | bytes 44293120 | tf_op jit(solution)/shard_map/convert_element_type | solution.py:33
  116.3 4.6 %fusion.7 = bf16[4096,896]{1,0:T(8,128)(2,1)} fusion(bf16[4096,896]{1,0:T(8,128)(2,1)S(1)} %get-tuple-element.8, f32[32,896]{1,0:T(8,128)S(1)} %get-tuple-element.14), kind=kLoop, calls=%fused_computation.11 | loop fusion | flops 11010048 | bytes 14794752 | tf_op jit(solution)/shard_map/convert_element_type | solution.py:38
  120.8 8.4 %all-to-all-start.1 = ((bf16[32,128,896]{2,1,0:T(8,128)(2,1)}), bf16[32,128,896]{2,1,0:T(8,128)(2,1)}, u32[]{:S(2)}, u32[]{:S(2)}) async-start(bf16[32,128,896]{2,1,0:T(8,128)(2,1)} %bitcast.47), calls=%async_computation.1 | async-start | bytes 14680064 | tf_op jit(solution)/shard_map/all_to_all | solution.py:61
  129.2 7.5 %fusion.3 = bf16[4096,896]{1,0:T(8,128)(2,1)} fusion(bf16[4096,896]{1,0:T(8,128)(2,1)} %get-tuple-element.7, f32[32,896]{1,0:T(8,128)S(1)} %get-tuple-element.13), kind=kLoop, calls=%fused_computation.7 | loop fusion | flops 11010048 | bytes 14794752 | tf_op jit(solution)/shard_map/convert_element_type | solution.py:38
  136.7 116.7 %all-to-all-done.1 = bf16[32,128,896]{2,1,0:T(8,128)(2,1)} async-done(((bf16[32,128,896]{2,1,0:T(8,128)(2,1)}), bf16[32,128,896]{2,1,0:T(8,128)(2,1)}, u32[]{:S(2)}, u32[]{:S(2)}) %all-to-all-start.1) | async-done | bytes 7340064 | tf_op jit(solution)/shard_map/all_to_all | solution.py:61
  253.4 7.9 %all-to-all-start = ((bf16[32,128,896]{2,1,0:T(8,128)(2,1)}), bf16[32,128,896]{2,1,0:T(8,128)(2,1)}, u32[]{:S(2)}, u32[]{:S(2)}) async-start(bf16[32,128,896]{2,1,0:T(8,128)(2,1)} %bitcast.46), calls=%async_computation | async-start | bytes 14680064 | tf_op jit(solution)/shard_map/all_to_all | solution.py:61
  261.3 4.2 %convert_reduce_fusion = f32[128,896]{1,0:T(8,128)S(1)} fusion(bf16[32,128,896]{2,1,0:T(8,128)(2,1)} %bitcast.12), kind=kLoop, calls=%fused_computation.12 | loop fusion | flops 7225344 | bytes 7798784 | tf_op jit(solution)/shard_map/reduce_sum | solution.py:63
  265.5 106.0 %all-to-all-done = bf16[32,128,896]{2,1,0:T(8,128)(2,1)} async-done(((bf16[32,128,896]{2,1,0:T(8,128)(2,1)}), bf16[32,128,896]{2,1,0:T(8,128)(2,1)}, u32[]{:S(2)}, u32[]{:S(2)}) %all-to-all-start) | async-done | bytes 7340064 | tf_op jit(solution)/shard_map/all_to_all | solution.py:61
  371.5 4.2 %convert_reduce_fusion.1 = f32[128,896]{1,0:T(8,128)S(1)} fusion(bf16[32,128,896]{2,1,0:T(8,128)(2,1)} %bitcast.11), kind=kLoop, calls=%fused_computation.13 | loop fusion | flops 7225344 | bytes 7798784 | tf_op jit(solution)/shard_map/reduce_sum | solution.py:63
  375.6 1.0 pad_maximum_fusion
  (3 shorter events, 0.1 us)
Async XLA Ops:
  6.5 2.6 copy-start
  6.5 79.4 %all-gather.2.cloned.1.call-start = ((), (), s32[]{:S(2)}) async-start(), calls=%async_computation.2 | async-start | bytes 7077888 | tf_op jit(solution)/shard_map/all_gather | solution.py:44
  7.9 5.6 %copy-start.2 = (f32[1,1792]{1,0:T(1,128)S(1)}, f32[1,1792]{1,0:T(1,128)}, u32[]{:S(2)}) copy-start(f32[1,1792]{1,0:T(1,128)} %param.8) | copy-start | bytes 21508
  13.6 82.3 %copy-start.4 = (bf16[768,1792]{1,0:T(8,128)(2,1)S(1)}, bf16[768,1792]{1,0:T(8,128)(2,1)}, u32[]{:S(2)}) copy-start(bf16[768,1792]{1,0:T(8,128)(2,1)} %param.6) | copy-start | bytes 8257540
  85.9 10.0 %copy-start.3 = (bf16[768,4096]{1,0:T(8,128)(2,1)S(1)}, bf16[768,4096]{1,0:T(8,128)(2,1)}, u32[]{:S(2)}) copy-start(bf16[768,4096]{1,0:T(8,128)(2,1)} %all-gather.2.cloned.1.call-done) | copy-start | bytes 18874372
  95.9 10.4 %copy-start.1 = (f32[1,4096]{1,0:T(1,128)S(1)}, f32[1,4096]{1,0:T(1,128)}, u32[]{:S(2)}) copy-start(f32[1,4096]{1,0:T(1,128)} %param.9) | copy-start | bytes 49156
  120.8 132.6 %all-to-all-start.1 = ((bf16[32,128,896]{2,1,0:T(8,128)(2,1)}), bf16[32,128,896]{2,1,0:T(8,128)(2,1)}, u32[]{:S(2)}, u32[]{:S(2)}) async-start(bf16[32,128,896]{2,1,0:T(8,128)(2,1)} %bitcast.47), calls=%async_computation.1 | async-start | bytes 14680064 | tf_op jit(solution)/shard_map/all_to_all | solution.py:61
  253.4 118.0 %all-to-all-start = ((bf16[32,128,896]{2,1,0:T(8,128)(2,1)}), bf16[32,128,896]{2,1,0:T(8,128)(2,1)}, u32[]{:S(2)}, u32[]{:S(2)}) async-start(bf16[32,128,896]{2,1,0:T(8,128)(2,1)} %bitcast.46), calls=%async_computation | async-start | bytes 14680064 | tf_op jit(solution)/shard_map/all_to_all | solution.py:61
Sparse Core Ops, SparseCore 0:
  13.6 72.2 all-gather.1
where the time goes:
time: 384 us; the launch traced here: 383 us
  waiting for transfers between devices  295 us (77%)
  other arithmetic  37.6 us (10%)
  matrix products  20.3 us (5%)
  starting transfers between devices  16.2 us (4%)
  between operations  13.5 us (4%)
    all_to_all x2, waiting for transfers between devices, per_device(): lax.all_to_all(terms, 'dp', split_axis=0, concat_axis=0, tiled=True)  223 us
    all_gather x1, waiting for transfers between devices, per_device(): y_hat = lax.all_gather(y_local, 'tensor', axis=0, tiled=True)  72.3 us
    dot_general x2, matrix products, per_device(): lax.dot_general(y_hat, activations[:, cols], (((0,), (0,)), ((), ())), pr...  20.3 us
    all_to_all x2, starting transfers between devices, per_device(): lax.all_to_all(terms, 'dp', split_axis=0, concat_axis=0, tiled=True)  16.2 us
    convert_element_type x2, other arithmetic, group_terms(): return values.reshape(feat_rows, unit_cols).astype(jnp.bfloat16)  12.1 us
    convert_element_type x1, other arithmetic, group_terms(): (scaled + hidden_part[None, :] + feature_part[:, None]).astype(jnp.bfloat16)  9.97 us
    reduce_sum x2, other arithmetic, per_device(): sums.append(jnp.sum(held.reshape(owners, own_rows, width), axis=0))  8.3 us
  transfers between devices with their start and end apart: 3, of which 3 were waited for; matrix products, arithmetic and copies ran while one was open for 3% of the time, Pallas kernels for 0%

commit v1 on v0

--- a/solution.py
+++ b/solution.py
@@ -2,12 +2,16 @@
 import jax.numpy as jnp
 from jax import lax
 from jax.sharding import PartitionSpec as P
+from jax.lax import all_to_all, axis_size
 
 BLOCK = 128
 Y_LEVELS = 8
 W_LEVELS = 7
 COL_CHUNKS = 2
 epsilon = 1e-06
+process_rails_on = lambda slab_in, dim_at: jnp.concatenate(
+    all_to_all(jnp.stack([slab_in] * axis_size("tensor")), "tensor", 0, 0), axis=dim_at
+)
 
 
 def code_rows(grad_out, grad_dither):
@@ -41,7 +45,7 @@
 def per_device(grad_out, activations, grad_dither, hidden_dither, feature_dither):
     feat_width = grad_out.shape[1]
     y_local = code_rows(grad_out, grad_dither)
-    y_hat = lax.all_gather(y_local, "tensor", axis=0, tiled=True)
+    y_hat = process_rails_on(y_local, dim_at=0)
     unit_count = activations.shape[1]
     owners = lax.axis_size("dp")
     own_rows = feat_width // owners

time: 384 us -> 462 us (1.20)
  waiting for transfers between devices: 295 us -> 349 us
  other arithmetic: 37.6 us -> 51.6 us
  between operations: 13.5 us -> 0.11 us
  local copies, waits for them, and re-layouts: 0.79 us -> 12.9 us
  starting transfers between devices: 16.2 us -> 23.9 us
    all_to_all x0 -> x1, waiting for transfers between devices: none -> 142 us  [all_to_all(jnp.stack([slab_in] * axis_size('tensor')), 'tensor', 0, 0)]
    all_gather x1 -> x0, waiting for transfers between devices: 72.3 us -> none  [per_device(): y_hat = lax.all_gather(y_local, 'tensor', axis=0, tiled=True)]
    all_to_all x2, waiting for transfers between devices: 223 us -> 207 us  [per_device(): lax.all_to_all(terms, 'dp', split_axis=0, concat_axis=0, tiled=True)]
    div x0 -> x1, other arithmetic: none -> 15.5 us  [group_terms(): blocks / block_scale.astype(jnp.float32)[:, None, :]]
    dot_general x0 -> x1, local copies, waits for them, and re-layouts: none -> 8.68 us  [per_device(): lax.dot_general(y_hat, activations[:, cols], (((0,), (0,)), ((), ())), pr...]
    all_to_all x0 -> x1, starting transfers between devices: none -> 7.7 us  [all_to_all(jnp.stack([slab_in] * axis_size('tensor')), 'tensor', 0, 0)]
where the time goes in v1:
time: 462 us
  waiting for transfers between devices  349 us (76%)
  other arithmetic  51.6 us (11%)
  matrix products  24.4 us (5%)
  starting transfers between devices  23.9 us (5%)
  local copies, waits for them, and re-layouts  12.9 us (3%)
    all_to_all x2, waiting for transfers between devices, per_device(): lax.all_to_all(terms, 'dp', split_axis=0, concat_axis=0, tiled=True)  207 us
    all_to_all x1, waiting for transfers between devices, all_to_all(jnp.stack([slab_in] * axis_size('tensor')), 'tensor', 0, 0)  142 us
    dot_general x2, matrix products, per_device(): lax.dot_general(y_hat, activations[:, cols], (((0,), (0,)), ((), ())), pr...  24.4 us
    all_to_all x2, starting transfers between devices, per_device(): lax.all_to_all(terms, 'dp', split_axis=0, concat_axis=0, tiled=True)  16.2 us
    div x1, other arithmetic, group_terms(): blocks / block_scale.astype(jnp.float32)[:, None, :]  15.5 us
    convert_element_type x2, other arithmetic, group_terms(): return values.reshape(feat_rows, unit_cols).astype(jnp.bfloat16)  12 us
  transfers between devices with their start and end apart: 3, of which 3 were waited for; matrix products, arithmetic and copies ran while one was open for 3% of the time, Pallas kernels for 0%

profile of v1, /device:TPU:38, one launch (start us, length us, event | category | flops | bytes accessed | tf_op | source)
XLA Modules:
  0.0 461.5 jit_solution(14424383071283690330)
XLA Ops:
  0.0 0.0 copy-start.1
  0.0 1.4 fusion.6
  1.4 0.3 copy.8
  1.7 0.5 reduce_max.27
  2.2 0.5 div.45
  2.6 0.0 copy-done.1
  2.6 2.5 fusion.8
  5.2 1.3 fusion.9
  6.4 3.4 stack.2
  9.9 0.0 copy-start.3
  9.9 7.7 %all-to-all-start = ((bf16[8,96,4096]{2,1,0:T(8,128)(2,1)}), bf16[8,96,4096]{2,1,0:T(8,128)(2,1)}, u32[]{:S(2)}, u32[]{:S(2)}) async-start(bf16[8,96,4096]{2,1,0:T(8,128)(2,1)} %stack.2), calls=%async_computation | async-start | bytes 12582912 | tf_op jit(solution)/shard_map/all_to_all | solution.py:13
  17.6 0.0 copy-done.3
  17.6 0.0 copy-start.4
  17.6 141.7 %all-to-all-done = bf16[8,96,4096]{2,1,0:T(8,128)(2,1)} async-done(((bf16[8,96,4096]{2,1,0:T(8,128)(2,1)}), bf16[8,96,4096]{2,1,0:T(8,128)(2,1)}, u32[]{:S(2)}, u32[]{:S(2)}) %all-to-all-start) | async-done | bytes 6291488 | tf_op jit(solution)/shard_map/all_to_all | solution.py:13
  159.3 8.7 %copy.7 = bf16[4096,768]{1,0:T(8,128)(2,1)} copy(bf16[4096,768]{0,1:T(8,128)(2,1)} %bitcast.1) | data formatting | bytes 12582912 | tf_op jit(solution)/shard_map/dot_general | solution.py:58
  168.0 0.0 copy-done.4
  168.0 0.0 copy-start
  168.0 14.0 %abs_reduce_fusion.1 = (f32[32,896]{1,0:T(8,128)S(1)}, f32[32,128,896]{2,1,0:T(8,128)}) fusion(bf16[32,128,768]{2,1,0:T(8,128)(2,1)} %bitcast.58, bf16[768,1792]{1,0:T(8,128)(2,1)S(1)} %copy-done.4), kind=kOutput, calls=%fused_computation.13 | convolution fusion | flops 5644455936 | bytes 22462464 | tf_op jit(solution)/shard_map/dot_general | solution.py:58
  182.0 0.0 copy-done
  182.0 10.4 %abs_reduce_fusion = (f32[32,896]{1,0:T(8,128)S(1)}, f32[32,128,896]{2,1,0:T(8,128)}) fusion(bf16[32,128,768]{2,1,0:T(8,128)(2,1)S(1)} %bitcast.59, bf16[768,1792]{1,0:T(8,128)(2,1)S(1)} %copy-done.4), kind=kOutput, calls=%fused_computation.12 | convolution fusion | flops 5644455936 | bytes 22462464 | tf_op jit(solution)/shard_map/dot_general | solution.py:58
  192.4 0.0 copy-start.2
  192.4 15.5 %broadcast_divide_fusion = (f32[32,128,896]{2,1,0:T(8,128)S(1)}, f32[32,128,896]{2,1,0:T(8,128)}) fusion(f32[32,128,896]{2,1,0:T(8,128)} %get-tuple-element.12, f32[32,896]{1,0:T(8,128)S(1)} %fusion.17, f32[32,128,896]{2,1,0:T(8,128)} %get-tuple-element.10, f32[32,896]{1,0:T(8,128)S(1)} %fusion.16), kind=kLoop, calls=%fused_computation.14 | loop fusion | flops 7340032 | bytes 58949632 | tf_op jit(solution)/shard_map/div | solution.py:36
  207.9 0.0 copy-done.2
  207.9 9.2 %fusion.5 = (bf16[4096,896]{1,0:T(8,128)(2,1)S(1)}, bf16[4096,896]{1,0:T(8,128)(2,1)}) fusion(f32[32,128,896]{2,1,0:T(8,128)} %get-tuple-element.14, f32[4096]{0:T(1024)S(1)} %bitcast.61, f32[896]{0:T(1024)S(1)} %get-tuple-element.5, f32[896]{0:T(1024)S(1)} %get-tuple-element.6, f32[32,128,896]{2,1,0:T(8,128)S(1)} %get-tuple-element.13), kind=kLoop, calls=%fused_computation.11 | loop fusion | flops 22020096 | bytes 44063744 | tf_op jit(solution)/shard_map/convert_element_type | solution.py:37
  217.1 4.6 fusion.3
  221.6 8.5 %all-to-all-start.1 = ((bf16[32,128,896]{2,1,0:T(8,128)(2,1)}), bf16[32,128,896]{2,1,0:T(8,128)(2,1)}, u32[]{:S(2)}, u32[]{:S(2)}) async-start(bf16[32,128,896]{2,1,0:T(8,128)(2,1)} %bitcast.55), calls=%async_computation.1 | async-start | bytes 14680064 | tf_op jit(solution)/shard_map/all_to_all | solution.py:65
  230.2 7.5 %fusion = bf16[4096,896]{1,0:T(8,128)(2,1)} fusion(bf16[4096,896]{1,0:T(8,128)(2,1)} %get-tuple-element.8, f32[32,896]{1,0:T(8,128)S(1)} %fusion.17), kind=kLoop, calls=%fused_computation.3 | loop fusion | flops 11010048 | bytes 14794752 | tf_op jit(solution)/shard_map/convert_element_type | solution.py:42
  237.6 106.1 %all-to-all-done.1 = bf16[32,128,896]{2,1,0:T(8,128)(2,1)} async-done(((bf16[32,128,896]{2,1,0:T(8,128)(2,1)}), bf16[32,128,896]{2,1,0:T(8,128)(2,1)}, u32[]{:S(2)}, u32[]{:S(2)}) %all-to-all-start.1) | async-done | bytes 7340064 | tf_op jit(solution)/shard_map/all_to_all | solution.py:65
  343.7 7.7 %all-to-all-start.2 = ((bf16[32,128,896]{2,1,0:T(8,128)(2,1)}), bf16[32,128,896]{2,1,0:T(8,128)(2,1)}, u32[]{:S(2)}, u32[]{:S(2)}) async-start(bf16[32,128,896]{2,1,0:T(8,128)(2,1)} %bitcast.54), calls=%async_computation.2 | async-start | bytes 14680064 | tf_op jit(solution)/shard_map/all_to_all | solution.py:65
  351.4 4.2 convert_reduce_fusion.1
  355.6 100.8 %all-to-all-done.2 = bf16[32,128,896]{2,1,0:T(8,128)(2,1)} async-done(((bf16[32,128,896]{2,1,0:T(8,128)(2,1)}), bf16[32,128,896]{2,1,0:T(8,128)(2,1)}, u32[]{:S(2)}, u32[]{:S(2)}) %all-to-all-start.2) | async-done | bytes 7340064 | tf_op jit(solution)/shard_map/all_to_all | solution.py:65
  456.4 4.2 convert_reduce_fusion
  460.5 1.0 pad_maximum_fusion
  (4 shorter events, 0.1 us)
Async XLA Ops:
  0.0 2.6 copy-start.1
  9.9 7.7 %copy-start.3 = (f32[1,1792]{1,0:T(1,128)S(1)}, f32[1,1792]{1,0:T(1,128)}, u32[]{:S(2)}) copy-start(f32[1,1792]{1,0:T(1,128)} %param.8) | copy-start | bytes 21508
  9.9 149.4 %all-to-all-start = ((bf16[8,96,4096]{2,1,0:T(8,128)(2,1)}), bf16[8,96,4096]{2,1,0:T(8,128)(2,1)}, u32[]{:S(2)}, u32[]{:S(2)}) async-start(bf16[8,96,4096]{2,1,0:T(8,128)(2,1)} %stack.2), calls=%async_computation | async-start | bytes 12582912 | tf_op jit(solution)/shard_map/all_to_all | solution.py:13
  17.6 150.4 %copy-start.4 = (bf16[768,1792]{1,0:T(8,128)(2,1)S(1)}, bf16[768,1792]{1,0:T(8,128)(2,1)}, u32[]{:S(2)}) copy-start(bf16[768,1792]{1,0:T(8,128)(2,1)} %param.6) | copy-start | bytes 8257540
  168.0 14.0 %copy-start = (bf16[4096,768]{1,0:T(8,128)(2,1)S(1)}, bf16[4096,768]{1,0:T(8,128)(2,1)}, u32[]{:S(2)}) copy-start(bf16[4096,768]{1,0:T(8,128)(2,1)} %copy.7) | copy-start | bytes 18874372
  192.4 15.5 %copy-start.2 = (f32[1,4096]{1,0:T(1,128)S(1)}, f32[1,4096]{1,0:T(1,128)}, u32[]{:S(2)}) copy-start(f32[1,4096]{1,0:T(1,128)} %param.9) | copy-start | bytes 49156
  221.6 122.1 %all-to-all-start.1 = ((bf16[32,128,896]{2,1,0:T(8,128)(2,1)}), bf16[32,128,896]{2,1,0:T(8,128)(2,1)}, u32[]{:S(2)}, u32[]{:S(2)}) async-start(bf16[32,128,896]{2,1,0:T(8,128)(2,1)} %bitcast.55), calls=%async_computation.1 | async-start | bytes 14680064 | tf_op jit(solution)/shard_map/all_to_all | solution.py:65
  343.7 112.7 %all-to-all-start.2 = ((bf16[32,128,896]{2,1,0:T(8,128)(2,1)}), bf16[32,128,896]{2,1,0:T(8,128)(2,1)}, u32[]{:S(2)}, u32[]{:S(2)}) async-start(bf16[32,128,896]{2,1,0:T(8,128)(2,1)} %bitcast.54), calls=%async_computation.2 | async-start | bytes 14680064 | tf_op jit(solution)/shard_map/all_to_all | solution.py:65
